TPU v7x, 32 devices: a whole 2x2x4 slice. The times are simulated.
32 devices in a mesh: dp: 4 (over y, x), tensor: 8 (over z, core).
Axes of the slice: x: 2, y: 2, z: 4, core: 2. Of those that a mesh axis runs over, the one named last changes fastest.
Arguments:
- hidden_act: bfloat16 [2816, 36864], P('dp', 'tensor'), may hold values from -80 to 80
- out_grad: bfloat16 [2816, 4608], P('dp', 'tensor'), may hold values from -0.5 to 0.5
- other_sq: float32 [8], P('dp'), may hold values from 2989699 to 597939968
Outputs:
- weight_grad: float32 [4608, 36864], P('dp', 'tensor')
All inputs are finite; a program needn't handle non-finite values.
Results may differ from a plain program's by a relative error of at most 0.002.
Values may be sent and summed in bfloat16 or wider, within the bound.
No kernel may reach another device: no remote copies, remote signals or barrier semaphores. Data moves between devices by JAX's collectives and lax.ppermute only.
A program may use at most 128 MiB of HBM per device.

v0:
```python
import math
import jax
import jax.numpy as jnp
from jax import lax
from jax.sharding import PartitionSpec as P

D = 4608
FF = 36864
L = 352


def on_device(hidden_act, out_grad, other_sq):
    examples_here = other_sq.shape[0]
    length = hidden_act.shape[0] // examples_here
    hidden_blocks = hidden_act.reshape(examples_here, length, hidden_act.shape[1])
    act_gram = jnp.einsum(
        "etf,esf->ets", hidden_blocks, hidden_blocks, preferred_element_type=jnp.float32
    )
    full_grad = lax.all_gather(out_grad, "tensor", axis=1, tiled=True)
    grad_blocks = full_grad.reshape(examples_here, length, full_grad.shape[1])
    local_blocks = out_grad.reshape(examples_here, length, out_grad.shape[1])
    grad_part = jnp.einsum(
        "etd,esd->ets", local_blocks, local_blocks, preferred_element_type=jnp.float32
    )
    act_total, grad_total = lax.psum((act_gram, grad_part), "tensor")
    layer_sq = jnp.sum(act_total * grad_total, axis=(1, 2))
    clip_bound = math.sqrt(L * FF * D / 80.0)
    clip_scale = jnp.minimum(1.0, clip_bound / jnp.sqrt(other_sq + layer_sq))
    scaled_grad = (grad_blocks.astype(jnp.float32) * clip_scale[:, None, None]).astype(jnp.bfloat16)
    scaled_grad = scaled_grad.reshape(examples_here * length, full_grad.shape[1])
    contract_rows = (((0,), (0,)), ((), ()))
    own_columns = lax.all_to_all(scaled_grad, "dp", split_axis=1, concat_axis=0, tiled=True)
    return lax.dot_general(
        own_columns,
        lax.all_gather(hidden_act, "dp", axis=0, tiled=True),
        contract_rows,
        preferred_element_type=jnp.float32,
    )


def solution(mesh):
    placed = (P("dp", "tensor"), P("dp", "tensor"), P("dp"))
    return jax.shard_map(
        on_device, mesh=mesh, in_specs=placed, out_specs=P("dp", "tensor"), check_vma=False
    )
```

profile of v0, /device:TPU:0, one launch (start us, length us, event | category | flops | bytes accessed | tf_op | source)
XLA Modules:
  0.0 509.5 jit_solution(13923911477526798754)
XLA Ops:
  6.5 0.0 all-reduce.3.cloned.1.call-start
  6.5 2.6 reshape.14
  9.2 1.7 fusion
  10.9 9.2 %fusion.2 = f32[2,352,352]{2,1,0:T(8,128)} fusion(bf16[2,352,4608]{2,1,0:T(8,128)(2,1)} %bitcast.16), kind=kOutput, calls=%fused_computation.6 | convolution fusion | flops 2283798528 | bytes 7479296 | tf_op jit(solution)/shard_map/etf,esf->ets/dot_general | solution.py:16
  20.1 0.0 copy-start
  20.1 0.0 all-reduce.3.cloned.1.call-update
  20.1 0.0 all-gather.3.cloned.1.call-start
  20.2 0.7 all-gather.3.cloned.1.call-update
  20.9 0.0 all-gather.5.cloned.1.call-start
  20.9 0.7 all-gather.5.cloned.1.call-update
  21.6 67.1 %all-reduce.3.cloned.1.call-done = (f32[2,352,352]{2,1,0:T(8,128)}, f32[2,352,352]{2,1,0:T(8,128)}) async-done(((f32[2,352,352]{2,1,0:T(8,128)}, f32[2,352,352]{2,1,0:T(8,128)}), (f32[2,352,352]{2,1,0:T(8,128)}, f32[2,352,352]{2,1,0:T(8,128)})) %all-reduce.3.cloned.1.call-update) | async-done | bytes 1982480 | tf_op jit(solution)/shard_map/psum | solution.py:25
  88.7 1.8 multiply_reduce_fusion
  90.5 0.0 copy-done
  90.5 0.1 mul.17
  90.6 0.1 mul.18
  90.7 70.5 %all-gather.3.cloned.1.call-done = bf16[704,4608]{0,1:T(8,128)(2,1)} async-done(((bf16[704,576]{0,1:T(8,128)(2,1)}), bf16[704,4608]{0,1:T(8,128)(2,1)}) %all-gather.3.cloned.1.call-update) | async-done | bytes 6488080 | tf_op jit(solution)/shard_map/all_gather | solution.py:19
  161.1 10.0 %copy.20 = bf16[704,4608]{1,0:T(8,128)(2,1)} copy(bf16[704,4608]{0,1:T(8,128)(2,1)} %all-gather.3.cloned.1.call-done) | data formatting | bytes 12976128 | tf_op jit(solution)/shard_map/all_gather | solution.py:19
  171.2 6.6 %multiply_convert_fusion = bf16[704,4608]{1,0:T(8,128)(2,1)S(1)} fusion(bf16[704,4608]{1,0:T(8,128)(2,1)} %copy.20, f32[704]{0:T(1024)S(1)} %mul.18), kind=kLoop, calls=%fused_computation | loop fusion | flops 9732096 | bytes 12978944 | tf_op jit(solution)/shard_map/convert_element_type | solution.py:29
  177.7 0.5 copy.28
  178.2 140.2 %all_to_all.19 = bf16[704,4,1152]{2,0,1:T(8,128)(2,1)} all-to-all(bf16[704,4,1152]{2,0,1:T(8,128)(2,1)S(1)} %bitcast.15), channel_id=1, replica_groups=mesh['dp'=4,'tensor'=8] {'dp'}, dimensions={1} | all-to-all | bytes 12976128 | tf_op jit(solution)/shard_map/all_to_all | solution.py:32
  318.4 146.8 %all-gather.5.cloned.1.call-done = bf16[2816,4608]{1,0:T(8,128)(2,1)} async-done(((bf16[704,4608]{1,0:T(8,128)(2,1)}), bf16[2816,4608]{1,0:T(8,128)(2,1)}) %all-gather.5.cloned.1.call-update) | async-done | bytes 25952272 | tf_op jit(solution)/shard_map/all_gather | solution.py:35
  465.2 37.7 %fusion.3 = f32[1152,4608]{1,0:T(8,128)} fusion(bf16[2816,1152]{1,0:T(8,128)(2,1)} %bitcast.17, bf16[2816,4608]{1,0:T(8,128)(2,1)} %all-gather.5.cloned.1.call-done), kind=kOutput, calls=%fused_computation.7 | convolution fusion | flops 29896998912 | bytes 53673984 | tf_op jit(solution)/shard_map/dot_general | solution.py:33
  (1 shorter events, 0.0 us)
Async XLA Ops:
  6.5 82.2 %all-reduce.3.cloned.1.call-start = ((), (), s32[]{:S(2)}) async-start(), calls=%async_computation.3 | async-start | bytes 4325376 | tf_op jit(solution)/shard_map/psum | solution.py:25
  20.1 70.4 %copy-start = (f32[2]{0:T(128)S(1)}, f32[2]{0:T(128)}, u32[]{:S(2)}) copy-start(f32[2]{0:T(128)} %param.5) | copy-start | bytes 28
  20.1 141.0 %all-gather.3.cloned.1.call-start = ((), (), s32[]{:S(2)}) async-start(), calls=%async_computation.1 | async-start | bytes 7962624 | tf_op jit(solution)/shard_map/all_gather | solution.py:19
  20.9 444.3 %all-gather.5.cloned.1.call-start = ((), (), s32[]{:S(2)}) async-start(), calls=%async_computation.2 | async-start | bytes 32440320 | tf_op jit(solution)/shard_map/all_gather | solution.py:35
Sparse Core Ops, SparseCore 0:
  20.2 68.4 all-reduce.2
  90.3 70.7 all-gather.2
  163.0 302.1 all-gather.4
where the time goes:
time: 510 us; the launch traced here: 509 us
  waiting for transfers between devices  286 us (56%)
  blocking collectives  140 us (27%)
  matrix products  48.6 us (10%)
  local copies, waits for them, and re-layouts  13.3 us (3%)
  between operations  13.1 us (3%)
  other arithmetic  8.38 us (2%)
    all_gather x1, waiting for transfers between devices, on_device(): lax.all_gather(hidden_act, 'dp', axis=0, tiled=True)  147 us
    all_to_all x1, blocking collectives, on_device(): lax.all_to_all(scaled_grad, 'dp', split_axis=1, concat_axis=0, tiled=True)  140 us
    all_gather x1, waiting for transfers between devices, on_device(): full_grad = lax.all_gather(out_grad, 'tensor', axis=1, tiled=True)  70.5 us
    psum x1, waiting for transfers between devices, on_device(): act_total, grad_total = lax.psum((act_gram, grad_part), 'tensor')  67.1 us
    dot_general x1, matrix products, on_device(): lax.dot_general(own_columns, lax.all_gather(hidden_act, 'dp', axis=0, til...  37.7 us
  transfers between devices with their start and end apart: 3, of which 3 were waited for; matrix products, arithmetic and copies ran while one was open for 4% of the time, Pallas kernels for 0%

commit v1 on v0

--- a/solution.py
+++ b/solution.py
@@ -16,7 +16,22 @@
     act_gram = jnp.einsum(
         "etf,esf->ets", hidden_blocks, hidden_blocks, preferred_element_type=jnp.float32
     )
-    full_grad = lax.all_gather(out_grad, "tensor", axis=1, tiled=True)
+
+    def racks_wait(payload, link_axis):
+        all_values, g_now = (lax.axis_size(link_axis), lax.axis_index(link_axis))
+        response, piece_next = (payload, 1)
+        while piece_next < all_values:
+            inbox = []
+            for no in range(all_values):
+                inbox.append((no, no ^ piece_next))
+            local_part = lax.ppermute(response, axis_name=link_axis, perm=inbox)
+            near = jnp.concatenate([response, local_part], axis=1)
+            y_new = jnp.concatenate([local_part, response], axis=1)
+            response = jnp.where(g_now & piece_next == 0, near, y_new)
+            piece_next = 2 * piece_next
+        return response
+
+    full_grad = racks_wait(out_grad, "tensor")
     grad_blocks = full_grad.reshape(examples_here, length, full_grad.shape[1])
     local_blocks = out_grad.reshape(examples_here, length, out_grad.shape[1])
     grad_part = jnp.einsum(

time: 510 us -> 376 us (0.74)
  waiting for transfers between devices: 286 us -> 206 us
  blocking collectives: 140 us -> 78.2 us
  starting transfers between devices: 0.08 us -> 5.97 us
    all_gather x1, waiting for transfers between devices: 147 us -> 0.01 us  [on_device(): lax.all_gather(hidden_act, 'dp', axis=0, tiled=True)]
    ppermute x0 -> x3, waiting for transfers between devices: none -> 123 us  [racks_wait(): local_part = lax.ppermute(response, axis_name=link_axis, perm=inbox)]
    all_gather x1 -> x0, waiting for transfers between devices: 70.5 us -> none  [on_device(): full_grad = lax.all_gather(out_grad, 'tensor', axis=1, tiled=True)]
    all_to_all x1, blocking collectives: 140 us -> 78.2 us  [on_device(): lax.all_to_all(scaled_grad, 'dp', split_axis=1, concat_axis=0, tiled=True)]
    psum x1, waiting for transfers between devices: 67.1 us -> 82.3 us  [on_device(): act_total, grad_total = lax.psum((act_gram, grad_part), 'tensor')]
    all_gather x1 -> x0, local copies, waits for them, and re-layouts: 10 us -> none  [on_device(): full_grad = lax.all_gather(out_grad, 'tensor', axis=1, tiled=True)]
    select_n x0 -> x4, other arithmetic: none -> 9.07 us  [racks_wait(): response = jnp.where(g_now & piece_next == 0, near, y_new)]
    ppermute x0 -> x3, starting transfers between devices: none -> 5.93 us  [racks_wait(): local_part = lax.ppermute(response, axis_name=link_axis, perm=inbox)]
  transfers between devices with their start and end apart: 3 -> 5, of which waited for: 3 -> 4; matrix products, arithmetic and copies ran while one was open for 4% -> 5% of each run, Pallas kernels for 0% -> 0%
where the time goes in v1:
time: 376 us; the launch traced here: 375 us
  waiting for transfers between devices  206 us (55%)
  blocking collectives  78.2 us (21%)
  matrix products  48.7 us (13%)
  between operations  14.9 us (4%)
  other arithmetic  13.2 us (4%)
  local copies, waits for them, and re-layouts  8.41 us (2%)
  starting transfers between devices  5.97 us (2%)
    ppermute x3, waiting for transfers between devices, racks_wait(): local_part = lax.ppermute(response, axis_name=link_axis, perm=inbox)  123 us
    psum x1, waiting for transfers between devices, on_device(): act_total, grad_total = lax.psum((act_gram, grad_part), 'tensor')  82.3 us
    all_to_all x1, blocking collectives, on_device(): lax.all_to_all(scaled_grad, 'dp', split_axis=1, concat_axis=0, tiled=True)  78.2 us
    dot_general x1, matrix products, on_device(): lax.dot_general(own_columns, lax.all_gather(hidden_act, 'dp', axis=0, til...  37.7 us
    dot_general x1, matrix products, on_device(): jnp.einsum('etf,esf->ets', hidden_blocks, hidden_blocks, preferred_elemen...  9.23 us
    select_n x4, other arithmetic, racks_wait(): response = jnp.where(g_now & piece_next == 0, near, y_new)  9.07 us
  transfers between devices with their start and end apart: 5, of which 4 were waited for; matrix products, arithmetic and copies ran while one was open for 5% of the time, Pallas kernels for 0%

profile of v1, /device:TPU:0, one launch (start us, length us, event | category | flops | bytes accessed | tf_op | source)
XLA Modules:
  0.0 375.3 jit_solution(245679214048294830)
XLA Ops:
  7.4 0.0 all-reduce.3.cloned.1.call-start
  7.4 2.6 reshape.64
  10.0 1.7 fusion
  11.7 9.2 %fusion.2 = f32[2,352,352]{2,1,0:T(8,128)} fusion(bf16[2,352,4608]{2,1,0:T(8,128)(2,1)} %bitcast.20), kind=kOutput, calls=%fused_computation.11 | convolution fusion | flops 2283798528 | bytes 7479296 | tf_op jit(solution)/shard_map/etf,esf->ets/dot_general | solution.py:16
  21.0 0.0 all-reduce.3.cloned.1.call-update
  21.0 0.0 copy-start.1
  21.0 0.0 all-gather.2.cloned.1.call-start
  21.1 0.5 all-gather.2.cloned.1.call-update
  21.6 0.6 copy-done.1
  22.2 0.5 collective-permute-start
  22.7 1.0 copy.29
  23.7 1.2 collective-permute-done
  24.9 1.9 copy.30
  26.7 2.3 maximum_select_fusion.4
  29.1 2.9 collective-permute-start.1
  32.0 61.2 %collective-permute-done.1 = bf16[704,1152]{1,0:T(8,128)(2,1)S(1)} collective-permute-done((bf16[704,1152]{1,0:T(8,128)(2,1)}, bf16[704,1152]{1,0:T(8,128)(2,1)S(1)}, u32[]{:S(2)}, u32[]{:S(2)}) %collective-permute-start.1) | collective-permute-done | bytes 1622048 | tf_op jit(solution)/shard_map/ppermute | solution.py:27
  93.2 3.8 %maximum_select_fusion.2 = bf16[704,2304]{1,0:T(8,128)(2,1)} fusion(bf16[704,1152]{1,0:T(8,128)(2,1)S(1)} %collective-permute-done.1, bf16[704,1152]{1,0:T(8,128)(2,1)} %maximum_select_fusion.4, pred[]{:T(512)S(6)} %eq.10), kind=kLoop, calls=%fused_computation.4 | loop fusion | flops 14598144 | bytes 6488065 | tf_op jit(solution)/shard_map/jit(_where)/select_n | solution.py:30
  97.0 0.0 copy-start.2
  97.0 2.5 collective-permute-start.2
  99.5 2.4 maximum_select_fusion.3
  101.9 82.3 %all-reduce.3.cloned.1.call-done = (f32[2,352,352]{2,1,0:T(8,128)}, f32[2,352,352]{2,1,0:T(8,128)}) async-done(((f32[2,352,352]{2,1,0:T(8,128)}, f32[2,352,352]{2,1,0:T(8,128)}), (f32[2,352,352]{2,1,0:T(8,128)}, f32[2,352,352]{2,1,0:T(8,128)})) %all-reduce.3.cloned.1.call-update) | async-done | bytes 1982480 | tf_op jit(solution)/shard_map/psum | solution.py:40
  184.2 1.8 multiply_reduce_fusion
  186.0 0.0 copy-done.2
  186.0 0.1 mul.18
  186.1 0.1 mul.19
  186.2 0.0 copy-done
  186.2 0.6 maximum_select_fusion.1
  186.8 60.7 %collective-permute-done.2 = bf16[704,2304]{1,0:T(8,128)(2,1)} collective-permute-done((bf16[704,2304]{1,0:T(8,128)(2,1)}, bf16[704,2304]{1,0:T(8,128)(2,1)}, u32[]{:S(2)}, u32[]{:S(2)}) %collective-permute-start.2) | collective-permute-done | bytes 3244064 | tf_op jit(solution)/shard_map/ppermute | solution.py:27
  247.5 2.2 copy.43
  249.6 2.3 multiply_convert_fusion
  251.9 78.2 %all_to_all.16 = bf16[704,4,1152]{2,0,1:T(8,128)(2,1)} all-to-all(bf16[704,4,1152]{2,0,1:T(8,128)(2,1)S(1)} %multiply_convert_fusion), channel_id=1, replica_groups=mesh['dp'=4,'tensor'=8] {'dp'}, dimensions={1} | all-to-all | bytes 12976128 | tf_op jit(solution)/shard_map/all_to_all | solution.py:47
  330.2 37.7 %fusion.3 = f32[1152,4608]{1,0:T(8,128)} fusion(bf16[2816,1152]{1,0:T(8,128)(2,1)} %bitcast.21, bf16[2816,4608]{1,0:T(8,128)(2,1)} %all-gather.2.cloned.1.call-done), kind=kOutput, calls=%fused_computation.12 | convolution fusion | flops 29896998912 | bytes 53673984 | tf_op jit(solution)/shard_map/dot_general | solution.py:48
  (3 shorter events, 0.0 us)
Async XLA Ops:
  7.4 176.8 %all-reduce.3.cloned.1.call-start = ((), (), s32[]{:S(2)}) async-start(), calls=%async_computation.2 | async-start | bytes 4325376 | tf_op jit(solution)/shard_map/psum | solution.py:40
  21.0 1.2 copy-start.1
  21.0 309.1 %all-gather.2.cloned.1.call-start = ((), (), s32[]{:S(2)}) async-start(), calls=%async_computation.1 | async-start | bytes 32440320 | tf_op jit(solution)/shard_map/all_gather | solution.py:50
  22.2 2.7 collective-permute-start
  29.1 64.1 %collective-permute-start.1 = (bf16[704,1152]{1,0:T(8,128)(2,1)}, bf16[704,1152]{1,0:T(8,128)(2,1)S(1)}, u32[]{:S(2)}, u32[]{:S(2)}) collective-permute-start(bf16[704,1152]{1,0:T(8,128)(2,1)} %maximum_select_fusion.4), channel_id=1, source_target_pairs={{0,2},{1,3},{2,0},{3,1},{4,6},{5,7},{6,4},{7,5},{8,10},{9,11},{10,... | collective-permute-start | bytes 4866056 | tf_op jit(solution)/shard_map/ppermute | solution.py:27
  97.0 89.0 %copy-start.2 = (f32[2]{0:T(128)S(1)}, f32[2]{0:T(128)}, u32[]{:S(2)}) copy-start(f32[2]{0:T(128)} %param.5) | copy-start | bytes 28
  97.0 150.5 %collective-permute-start.2 = (bf16[704,2304]{1,0:T(8,128)(2,1)}, bf16[704,2304]{1,0:T(8,128)(2,1)}, u32[]{:S(2)}, u32[]{:S(2)}) collective-permute-start(bf16[704,2304]{1,0:T(8,128)(2,1)} %maximum_select_fusion.2), channel_id=1, source_target_pairs={{0,4},{1,5},{2,6},{3,7},{4,0},{5,1},{6,2},{7,3},{8,12},{9,13},{10,... | collective-permute-start | bytes 9732104 | tf_op jit(solution)/shard_map/ppermute | solution.py:27
  101.9 84.3 %copy-start = (bf16[704,1,1152]{2,0,1:T(8,128)(2,1)S(1)}, bf16[704,1,1152]{2,0,1:T(8,128)(2,1)}, u32[]{:S(2)}) copy-start(bf16[704,1,1152]{2,0,1:T(8,128)(2,1)} %maximum_select_fusion.3) | copy-start | bytes 4866052
Sparse Core Ops, SparseCore 0:
  21.1 163.0 all-reduce.2
Sparse Core Ops, SparseCore 1:
  23.4 239.4 all-gather.1
